TPU v7x, 256 devices: a whole 4x4x8 slice. The times are simulated.
256 devices in a mesh: kern: 4 (over z_lo, core), slab: 64 (over z_hi, y, x).
Axes of the slice: x: 4, y: 4, z: 8 (z_hi: 4, z_lo: 2; z = z_hi * 2 + z_lo), core: 2. Of those that a mesh axis runs over, the one named last changes fastest.
Arguments:
- layout: int32 [4096, 4096], P('slab', 'kern'), may hold values 0 or 1
- band_freqs: int32 [128], replicated, may hold values from -256 to 255, as said below
- kernels: float32 [2, 48, 128, 128], P(None, 'kern'), may hold values from -6 to 6
- eigen_values: float32 [48], P('kern'), may hold values from 0.1 to 1
- bake_rates: float32 [5], replicated, may hold values from 0.1 to 0.25
Outputs:
- aerial_image: float32 [4096, 4096], P('slab', 'kern')
- latent_acid: float32 [4096, 4096], P('slab', 'kern')
Inputs may be any that keep to these rules, and one draw needn't show every extreme that they name: `band_freqs`: the 128 numbers are distinct; both ends of the range are among them.
All inputs are finite; a program needn't handle non-finite values. No bound on the sum of `layout` on one device may be relied on, other than what follows from the above.
Results may differ from a plain program's by a relative error of at most 0.0017.
Values sent between devices are 32-bit elements; how exact they have to be, the bound alone decides.
No kernel may reach another device: no remote copies, remote signals or barrier semaphores. Data moves between devices by JAX's collectives and lax.ppermute only.
A program may use at most 64 MiB of HBM per device.

v0:
```python
import math
import jax
import jax.numpy as jnp
from jax import lax
from jax.sharding import PartitionSpec as P

N = 4096
W = 128
FIELDS = 48
STEPS = 2
highest = lax.Precision.HIGHEST


def padded_2(cells, sides, width):
    for axis, dim in sides:
        count = lax.axis_size(axis)
        head = lax.slice_in_dim(cells, 0, width, axis=dim)
        tail = lax.slice_in_dim(cells, cells.shape[dim] - width, cells.shape[dim], axis=dim)
        cells = jnp.concatenate(
            [
                lax.ppermute(tail, axis, [(i, (i + 1) % count) for i in range(count)]),
                cells,
                lax.ppermute(head, axis, [((i + 1) % count, i) for i in range(count)]),
            ],
            axis=dim,
        )
    return cells


def tables(frequencies, first_index, length):
    positions = first_index + jnp.arange(length, dtype=jnp.int32)
    angles = jnp.mod(positions[:, None] * frequencies[None, :], N).astype(jnp.float32) * (
        2.0 * math.pi / N
    )
    return (jnp.cos(angles), jnp.sin(angles))


def stencil(padded):
    centre = padded[:, 1:-1, 1:-1]
    return (
        padded[:, 2:, 1:-1]
        + padded[:, :-2, 1:-1]
        + padded[:, 1:-1, 2:]
        + padded[:, 1:-1, :-2]
        - 4.0 * centre
    )


def bake(aerial_image, bake_rates, extend):
    dill_rate, acid_rate, quench_rate, react_rate, quench_start = (
        bake_rates[0],
        bake_rates[1],
        bake_rates[2],
        bake_rates[3],
        bake_rates[4],
    )
    acid_field = 1.0 - jnp.exp(-4.0 * dill_rate * aerial_image)
    acid_diffusion = acid_rate * (0.5 + 0.5 * acid_field)
    quencher = jnp.zeros_like(acid_field) + quench_start
    for bake_step in range(STEPS):
        laplaces = stencil(extend(jnp.stack([acid_field, quencher])))
        reaction = 4.0 * react_rate * acid_field * quencher
        new_acid = acid_field + acid_diffusion * laplaces[0] - reaction
        quencher = quencher + quench_rate * laplaces[1] - reaction
        acid_field = new_acid
    return acid_field


def shards(layout, band_freqs, kernels, eigen_values, bake_rates):
    rows = layout.shape[0]
    cols = layout.shape[1]
    row_first = lax.axis_index("slab") * rows
    col_first = lax.axis_index("kern") * cols
    transmit = (2 * layout - 1).astype(jnp.float32)
    cos_col, sin_col = tables(band_freqs, col_first, cols)
    along_re = jnp.dot(transmit, cos_col, precision=highest)
    along_im = -jnp.dot(transmit, sin_col, precision=highest)
    cos_row, sin_row = tables(band_freqs, row_first, rows)
    first = (
        jnp.dot(cos_row.T, along_re, precision=highest)
        + jnp.dot(sin_row.T, along_im, precision=highest)
    ) / N
    second = (
        jnp.dot(cos_row.T, along_im, precision=highest)
        - jnp.dot(sin_row.T, along_re, precision=highest)
    ) / N
    spectrum = lax.psum(jnp.stack([first, second]), ("kern", "slab"))
    spec_re = spectrum[0]
    spec_im = spectrum[1]
    row_table = jnp.concatenate([cos_row, sin_row], 1).astype(jnp.bfloat16)
    cos_all, sin_all = tables(band_freqs, 0, N)
    col_table = jnp.concatenate(
        [jnp.concatenate([cos_all.T, sin_all.T], 1), jnp.concatenate([-sin_all.T, cos_all.T], 1)], 0
    ).astype(jnp.bfloat16)

    def one_field(total_sum, field_item):
        kern_re, kern_im, eigen_one = field_item
        prod_re = spec_re * kern_re - spec_im * kern_im
        prod_im = spec_re * kern_im + spec_im * kern_re
        spectral_block = jnp.concatenate(
            [jnp.concatenate([prod_re, prod_im], 1), jnp.concatenate([-prod_im, prod_re], 1)], 0
        ).astype(jnp.bfloat16)
        row_field = (
            jnp.dot(row_table, spectral_block, preferred_element_type=jnp.float32) / W
        ).astype(jnp.bfloat16)
        field_pair = jnp.dot(row_field, col_table, preferred_element_type=jnp.float32)
        power = field_pair[:, :N] * field_pair[:, :N] + field_pair[:, N:] * field_pair[:, N:]
        return (total_sum + eigen_one * power, None)

    partial_sum, unused = lax.scan(
        one_field, jnp.zeros((rows, N), jnp.float32), (kernels[0], kernels[1], eigen_values)
    )
    whole_image = lax.psum(partial_sum, "kern") / FIELDS

    def extend_rows(stacked):
        padded = padded_2(stacked, (("slab", 1),), 1)
        return jnp.concatenate([padded[:, :, -1:], padded, padded[:, :, :1]], 2)

    whole_acid = bake(whole_image, bake_rates, extend_rows)
    aerial_image = lax.dynamic_slice_in_dim(whole_image, col_first, cols, 1)
    latent_acid = lax.dynamic_slice_in_dim(whole_acid, col_first, cols, 1)
    return (aerial_image, latent_acid)


def solution(mesh):
    return jax.shard_map(
        shards,
        mesh=mesh,
        in_specs=(P("slab", "kern"), P(), P(None, "kern", None, None), P("kern"), P()),
        out_specs=(P("slab", "kern"), P("slab", "kern")),
        check_vma=False,
    )
```

profile of v0, /device:TPU:32, one launch (start us, length us, event | category | flops | bytes accessed | tf_op | source)
XLA Modules:
  0.0 427.2 jit_solution(13018393930706624220)
XLA Ops:
  7.3 3.4 convolution_negate_fusion
  10.7 2.5 fusion.68
  16.3 9.7 %fusion.63 = (bf16[128,4096]{1,0:T(8,128)(2,1)S(1)}, bf16[128,4096]{1,0:T(8,128)(2,1)S(1)}, bf16[128,4096]{1,0:T(8,128)(2,1)}) fusion(s32[128]{0:T(128)S(1)} %copy-done.3), kind=kLoop, calls=%fused_computation.106 | loop fusion | flops 9437184 | bytes 3146240 | tf_op jit(solution)/shard_map/convert.11
  26.0 2.7 slice_bitcast_fusion.1
  28.6 12.2 %maximum_maximum_fusion = bf16[256,8192]{1,0:T(8,128)(2,1)} fusion(bf16[128,4096]{1,0:T(8,128)(2,1)} %get-tuple-element.122, bf16[128,4096]{1,0:T(8,128)(2,1)S(1)} %get-tuple-element.121, bf16[128,4096]{1,0:T(8,128)(2,1)S(1)} %get-tuple-element.120), kind=kLoop, calls=%fused_computation.26 | loop fusion | flops 16777216 | bytes 7340032 | tf_op jit(solution)/shard_map/concatenate | solution.py:92
  40.8 222.1 %all-reduce.4.cloned.1.call-done = f32[2,128,128]{2,1,0:T(8,128)} async-done(((f32[2,128,128]{2,1,0:T(8,128)}), f32[2,128,128]{2,1,0:T(8,128)}) %all-reduce.4.cloned.1.call-update) | async-done | bytes 131088 | tf_op jit(solution)/shard_map/psum | solution.py:87
  263.8 72.9 %while.11 = (s32[]{:T(128)}, f32[64,4096]{1,0:T(8,128)S(1)}, f32[12]{0:T(128)S(1)}, f32[12,128,128]{2,1,0:T(8,128)}, f32[128,128]{1,0:T(8,128)S(1)}, /*index=5*/...) while((s32[]{:T(128)}, f32[64,4096]{1,0:T(8,128)S(1)}, ...), condition=%wide.region_2.3_spmd.clone, body=%wide.region_1.2_spmd.clone.sunk | while | flops 279117824 | bytes 11108491 | solution.py:110
  264.8 3.3 fusion.143
  268.7 1.2 fusion.144
  270.8 3.3 fusion.143
  274.8 1.2 fusion.144
  276.9 3.3 fusion.143
  283.0 3.3 fusion.143
  289.1 3.3 fusion.143
  293.0 1.2 fusion.144
  295.1 3.3 fusion.143
  299.0 1.2 fusion.144
  301.2 3.3 fusion.143
  307.3 3.3 fusion.143
  313.3 3.3 fusion.143
  319.4 3.3 fusion.143
  325.5 3.3 fusion.143
  331.6 3.3 fusion.143
  339.1 42.2 %all-reduce.6.cloned.1.call-done = f32[64,4096]{1,0:T(8,128)} async-done(((f32[64,4096]{1,0:T(8,128)}), f32[64,4096]{1,0:T(8,128)}) %all-reduce.6.cloned.1.call-update) | async-done | bytes 1048592 | tf_op jit(solution)/shard_map/psum | solution.py:113
  381.3 2.1 add_multiply_fusion
  384.1 7.9 %collective-permute-start = (f32[2,1,4096]{2,1,0:T(1,128)S(1)}, f32[2,1,4096]{2,1,0:T(1,128)S(1)}, u32[]{:S(2)}, u32[]{:S(2)}) collective-permute-start(f32[2,1,4096]{2,1,0:T(1,128)S(1)} %get-tuple-element.110), channel_id=1, source_target_pairs={{1,0},{2,1},{3,2},{4,3},{5,4},{6,5},{7,6},{8,7},{9,8},{10,9},{11,1... | collective-permute-start | bytes 98312 | tf_op jit(solution)/shard_map/ppermute | solution.py:23
  393.6 8.8 %collective-permute-done.1 = f32[2,1,4096]{2,1,0:T(1,128)S(1)} collective-permute-done((f32[2,1,4096]{2,1,0:T(1,128)S(1)}, f32[2,1,4096]{2,1,0:T(1,128)S(1)}, u32[]{:S(2)}, u32[]{:S(2)}) %collective-permute-start.1) | collective-permute-done | bytes 32800 | tf_op jit(solution)/shard_map/ppermute | solution.py:21
  402.5 2.5 fusion.31
  405.0 2.4 fusion.61
  407.6 2.0 collective-permute-start.3
  411.5 6.4 %collective-permute-done.3 = f32[2,1,4096]{2,1,0:T(1,128)S(1)} collective-permute-done((f32[2,1,4096]{2,1,0:T(1,128)S(1)}, f32[2,1,4096]{2,1,0:T(1,128)S(1)}, u32[]{:S(2)}, u32[]{:S(2)}) %collective-permute-start.3) | collective-permute-done | bytes 32800 | tf_op jit(solution)/shard_map/ppermute | solution.py:21
  417.9 1.7 fusion.49
  (81 shorter events, 37.9 us)
Async XLA Ops:
  7.2 3.5 copy-start.4
  7.2 3.5 copy-start.3
  7.2 255.8 %all-reduce.4.cloned.1.call-start = ((), (), s32[]{:S(2)}) async-start(), calls=%async_computation | async-start | bytes 262144 | tf_op jit(solution)/shard_map/psum | solution.py:87
  15.8 365.5 %all-reduce.6.cloned.1.call-start = ((), (), s32[]{:S(2)}) async-start(), calls=%async_computation.1 | async-start | bytes 2097152 | tf_op jit(solution)/shard_map/psum | solution.py:113
  28.6 235.2 %copy-start.5 = (f32[12]{0:T(128)S(1)}, f32[12]{0:T(128)}, u32[]{:S(2)}) copy-start(f32[12]{0:T(128)} %param.10) | copy-start | bytes 148
  263.8 73.9 %copy-start.2 = (f32[5]{0:T(128)S(1)}, f32[5]{0:T(128)}, u32[]{:S(2)}) copy-start(f32[5]{0:T(128)} %param.11) | copy-start | bytes 64
  336.7 1.0 copy-start
  384.1 9.5 %collective-permute-start = (f32[2,1,4096]{2,1,0:T(1,128)S(1)}, f32[2,1,4096]{2,1,0:T(1,128)S(1)}, u32[]{:S(2)}, u32[]{:S(2)}) collective-permute-start(f32[2,1,4096]{2,1,0:T(1,128)S(1)} %get-tuple-element.110), channel_id=1, source_target_pairs={{1,0},{2,1},{3,2},{4,3},{5,4},{6,5},{7,6},{8,7},{9,8},{10,9},{11,1... | collective-permute-start | bytes 98312 | tf_op jit(solution)/shard_map/ppermute | solution.py:23
  392.0 10.4 %collective-permute-start.1 = (f32[2,1,4096]{2,1,0:T(1,128)S(1)}, f32[2,1,4096]{2,1,0:T(1,128)S(1)}, u32[]{:S(2)}, u32[]{:S(2)}) collective-permute-start(f32[2,1,4096]{2,1,0:T(1,128)S(1)} %get-tuple-element.109), channel_id=1, source_target_pairs={{0,1},{1,2},{2,3},{3,4},{4,5},{5,6},{6,7},{7,8},{8,9},{9,10},{10,1... | collective-permute-start | bytes 98312 | tf_op jit(solution)/shard_map/ppermute | solution.py:21
  393.4 11.6 %copy-start.1 = (f32[64,4096]{1,0:T(8,128)S(1)}, f32[64,4096]{1,0:T(8,128)}, u32[]{:S(2)}) copy-start(f32[64,4096]{1,0:T(8,128)} %all-reduce.6.cloned.1.call-done) | copy-start | bytes 3145732
  407.5 4.0 collective-permute-start.2
  407.6 10.3 %collective-permute-start.3 = (f32[2,1,4096]{2,1,0:T(1,128)S(1)}, f32[2,1,4096]{2,1,0:T(1,128)S(1)}, u32[]{:S(2)}, u32[]{:S(2)}) collective-permute-start(f32[2,1,4096]{2,1,0:T(1,128)S(1)} %get-tuple-element.103), channel_id=1, source_target_pairs={{0,1},{1,2},{2,3},{3,4},{4,5},{5,6},{6,7},{7,8},{8,9},{9,10},{10,1... | collective-permute-start | bytes 98312 | tf_op jit(solution)/shard_map/ppermute | solution.py:21
Sparse Core Ops, SparseCore 0:
  15.9 246.9 all-reduce.3
  337.8 43.4 all-reduce.5
where the time goes:
time: 429 us; the launch traced here: 427 us
  waiting for transfers between devices  281 us (66%)
  other arithmetic  58.7 us (14%)
  matrix products  47.6 us (11%)
  between operations  15.6 us (4%)
  local copies, waits for them, and re-layouts  13.8 us (3%)
  starting transfers between devices  10.2 us (2%)
    psum x1, waiting for transfers between devices, shards(): spectrum = lax.psum(jnp.stack([first, second]), ('kern', 'slab'))  222 us
    psum x1, waiting for transfers between devices, shards(): whole_image = lax.psum(partial_sum, 'kern') / FIELDS  42.2 us
    dot_general x12, matrix products, one_field(): jnp.dot(row_field, col_table, preferred_element_type=jnp.float32)  39.8 us
    another operation x26, other arithmetic  20.8 us
    ppermute x2, waiting for transfers between devices, padded_2(): lax.ppermute(tail, axis, [(i, (i + 1) % count) for i in range(count)])  15.3 us
    add x12, other arithmetic, one_field(): return (total_sum + eigen_one * power, None)  14.7 us
    concatenate x1, other arithmetic, shards(): jnp.concatenate([jnp.concatenate([cos_all.T, sin_all.T], 1), jnp.concaten...  12.2 us
  transfers between devices with their start and end apart: 6, of which 6 were waited for; matrix products, arithmetic and copies ran while one was open for 6% of the time, Pallas kernels for 0%

commit v1 on v0

--- a/solution.py
+++ b/solution.py
@@ -84,7 +84,7 @@
         jnp.dot(cos_row.T, along_im, precision=highest)
         - jnp.dot(sin_row.T, along_re, precision=highest)
     ) / N
-    spectrum = lax.psum(jnp.stack([first, second]), ("kern", "slab"))
+    spectrum = lax.psum(lax.psum(jnp.stack([first, second]), "slab"), "kern")
     spec_re = spectrum[0]
     spec_im = spectrum[1]
     row_table = jnp.concatenate([cos_row, sin_row], 1).astype(jnp.bfloat16)

time: 429 us -> 879 us (2.05)
  waiting for transfers between devices: 281 us -> 727 us
    psum x1 -> x2, waiting for transfers between devices: 222 us -> 665 us  [shards(): spectrum = lax.psum(lax.psum(jnp.stack([first, second]), 'slab'), 'kern')]
  transfers between devices with their start and end apart: 6 -> 7, of which waited for: 6 -> 7; matrix products, arithmetic and copies ran while one was open for 6% -> 4% of each run, Pallas kernels for 0% -> 0%
where the time goes in v1:
time: 879 us; the launch traced here: 878 us
  waiting for transfers between devices  727 us (83%)
  other arithmetic  64.4 us (7%)
  matrix products  47.6 us (5%)
  between operations  15.3 us (2%)
  local copies, waits for them, and re-layouts  12.4 us (1%)
  starting transfers between devices  10.5 us (1%)
    psum x2, waiting for transfers between devices, shards(): spectrum = lax.psum(lax.psum(jnp.stack([first, second]), 'slab'), 'kern')  665 us
    psum x1, waiting for transfers between devices, shards(): whole_image = lax.psum(partial_sum, 'kern') / FIELDS  45.7 us
    dot_general x12, matrix products, one_field(): jnp.dot(row_field, col_table, preferred_element_type=jnp.float32)  39.8 us
    another operation x26, other arithmetic  20.1 us
    concatenate x1, other arithmetic, shards(): jnp.concatenate([jnp.concatenate([cos_all.T, sin_all.T], 1), jnp.concaten...  18.6 us
  transfers between devices with their start and end apart: 7, of which 7 were waited for; matrix products, arithmetic and copies ran while one was open for 4% of the time, Pallas kernels for 0%

profile of v1, /device:TPU:32, one launch (start us, length us, event | category | flops | bytes accessed | tf_op | source)
XLA Modules:
  0.0 878.0 jit_solution(6567416712568292578)
XLA Ops:
  7.2 3.4 convolution_negate_fusion
  10.7 2.5 fusion.68
  16.0 9.0 %fusion.63 = (bf16[128,4096]{1,0:T(8,128)(2,1)S(1)}, bf16[128,4096]{1,0:T(8,128)(2,1)S(1)}, bf16[128,4096]{1,0:T(8,128)(2,1)S(1)}) fusion(s32[128]{0:T(128)S(1)} %copy-done.4), kind=kLoop, calls=%fused_computation.106 | loop fusion | flops 9437184 | bytes 3146240 | tf_op jit(solution)/shard_map/convert.11
  25.1 18.6 %maximum_maximum_fusion = bf16[256,8192]{1,0:T(8,128)(2,1)} fusion(bf16[128,4096]{1,0:T(8,128)(2,1)S(1)} %get-tuple-element.122, bf16[128,4096]{1,0:T(8,128)(2,1)S(1)} %get-tuple-element.121, bf16[128,4096]{1,0:T(8,128)(2,1)S(1)} %get-tuple-element.120), kind=kLoop, calls=%fused_computation.26 | loop fusion | flops 16777216 | bytes 7340032 | tf_op jit(solution)/shard_map/concatenate | solution.py:92
  43.7 1.3 slice_bitcast_fusion.1
  45.0 626.4 %all-reduce.5.cloned.1.call-done = f32[2,128,128]{2,1,0:T(8,128)} async-done(((f32[2,128,128]{2,1,0:T(8,128)}), f32[2,128,128]{2,1,0:T(8,128)}) %all-reduce.5.cloned.1.call-update) | async-done | bytes 131088 | tf_op jit(solution)/shard_map/psum | solution.py:87
  671.9 38.7 %all-reduce.7.cloned.1.call-done = f32[2,128,128]{2,1,0:T(8,128)} async-done(((f32[2,128,128]{2,1,0:T(8,128)}), f32[2,128,128]{2,1,0:T(8,128)}) %all-reduce.7.cloned.1.call-update) | async-done | bytes 131088 | tf_op jit(solution)/shard_map/psum | solution.py:87
  711.5 72.8 %while.11 = (s32[]{:T(128)}, f32[64,4096]{1,0:T(8,128)S(1)}, f32[12]{0:T(128)S(1)}, f32[12,128,128]{2,1,0:T(8,128)}, f32[128,128]{1,0:T(8,128)S(1)}, /*index=5*/...) while((s32[]{:T(128)}, f32[64,4096]{1,0:T(8,128)S(1)}, ...), condition=%wide.region_3.4_spmd.clone, body=%wide.region_2.3_spmd.clone.sunk | while | flops 279117824 | bytes 11108491 | solution.py:110
  712.5 3.3 fusion.143
  716.4 1.2 fusion.144
  718.5 3.3 fusion.143
  722.4 1.2 fusion.144
  724.6 3.3 fusion.143
  728.5 1.2 fusion.144
  730.7 3.3 fusion.143
  736.7 3.3 fusion.143
  742.8 3.3 fusion.143
  748.9 3.3 fusion.143
  754.9 3.3 fusion.143
  761.0 3.3 fusion.143
  767.1 3.3 fusion.143
  773.1 3.3 fusion.143
  779.2 3.3 fusion.143
  786.7 45.7 %all-reduce.9.cloned.1.call-done = f32[64,4096]{1,0:T(8,128)} async-done(((f32[64,4096]{1,0:T(8,128)}), f32[64,4096]{1,0:T(8,128)}) %all-reduce.9.cloned.1.call-update) | async-done | bytes 1048592 | tf_op jit(solution)/shard_map/psum | solution.py:113
  832.4 2.1 add_multiply_fusion
  835.2 7.9 collective-permute-start
  844.7 8.8 %collective-permute-done.1 = f32[2,1,4096]{2,1,0:T(1,128)S(1)} collective-permute-done((f32[2,1,4096]{2,1,0:T(1,128)S(1)}, f32[2,1,4096]{2,1,0:T(1,128)S(1)}, u32[]{:S(2)}, u32[]{:S(2)}) %collective-permute-start.1) | collective-permute-done | bytes 32800 | tf_op jit(solution)/shard_map/ppermute | solution.py:21
  853.6 2.5 fusion.31
  856.1 2.4 fusion.61
  858.7 2.0 collective-permute-start.3
  862.6 6.4 collective-permute-done.3
  869.0 1.7 fusion.49
  (86 shorter events, 39.3 us)
Async XLA Ops:
  7.2 3.5 copy-start.5
  7.2 3.5 copy-start.4
  7.2 664.2 %all-reduce.5.cloned.1.call-start = ((), (), s32[]{:S(2)}) async-start(), calls=%async_computation | async-start | bytes 262144 | tf_op jit(solution)/shard_map/psum | solution.py:87
  15.8 694.8 %all-reduce.7.cloned.1.call-start = ((), (), s32[]{:S(2)}) async-start(), calls=%async_computation.1 | async-start | bytes 262144 | tf_op jit(solution)/shard_map/psum | solution.py:87
  25.1 18.6 %copy-start.2 = (f32[2,12,128,128]{3,2,1,0:T(8,128)S(1)}, f32[2,12,128,128]{3,2,1,0:T(8,128)}, u32[]{:S(2)}) copy-start(f32[2,12,128,128]{3,2,1,0:T(8,128)} %param.9) | copy-start | bytes 4718596
  43.7 667.8 %copy-start.6 = (f32[12]{0:T(128)S(1)}, f32[12]{0:T(128)}, u32[]{:S(2)}) copy-start(f32[12]{0:T(128)} %param.10) | copy-start | bytes 148
  671.4 161.1 %all-reduce.9.cloned.1.call-start = ((), (), s32[]{:S(2)}) async-start(), calls=%async_computation.2 | async-start | bytes 2097152 | tf_op jit(solution)/shard_map/psum | solution.py:113
  711.5 73.8 %copy-start.3 = (f32[5]{0:T(128)S(1)}, f32[5]{0:T(128)}, u32[]{:S(2)}) copy-start(f32[5]{0:T(128)} %param.11) | copy-start | bytes 64
  784.4 1.0 copy-start
  835.2 9.5 %collective-permute-start = (f32[2,1,4096]{2,1,0:T(1,128)S(1)}, f32[2,1,4096]{2,1,0:T(1,128)S(1)}, u32[]{:S(2)}, u32[]{:S(2)}) collective-permute-start(f32[2,1,4096]{2,1,0:T(1,128)S(1)} %get-tuple-element.110), channel_id=1, source_target_pairs={{1,0},{2,1},{3,2},{4,3},{5,4},{6,5},{7,6},{8,7},{9,8},{10,9},{11,1... | collective-permute-start | bytes 98312 | tf_op jit(solution)/shard_map/ppermute | solution.py:23
  843.1 10.4 %collective-permute-start.1 = (f32[2,1,4096]{2,1,0:T(1,128)S(1)}, f32[2,1,4096]{2,1,0:T(1,128)S(1)}, u32[]{:S(2)}, u32[]{:S(2)}) collective-permute-start(f32[2,1,4096]{2,1,0:T(1,128)S(1)} %get-tuple-element.109), channel_id=1, source_target_pairs={{0,1},{1,2},{2,3},{3,4},{4,5},{5,6},{6,7},{7,8},{8,9},{9,10},{10,1... | collective-permute-start | bytes 98312 | tf_op jit(solution)/shard_map/ppermute | solution.py:21
  844.6 11.5 %copy-start.1 = (f32[64,4096]{1,0:T(8,128)S(1)}, f32[64,4096]{1,0:T(8,128)}, u32[]{:S(2)}) copy-start(f32[64,4096]{1,0:T(8,128)} %all-reduce.9.cloned.1.call-done) | copy-start | bytes 3145732
  858.6 4.0 collective-permute-start.2
  858.7 10.3 %collective-permute-start.3 = (f32[2,1,4096]{2,1,0:T(1,128)S(1)}, f32[2,1,4096]{2,1,0:T(1,128)S(1)}, u32[]{:S(2)}, u32[]{:S(2)}) collective-permute-start(f32[2,1,4096]{2,1,0:T(1,128)S(1)} %get-tuple-element.103), channel_id=1, source_target_pairs={{0,1},{1,2},{2,3},{3,4},{4,5},{5,6},{6,7},{7,8},{8,9},{9,10},{10,1... | collective-permute-start | bytes 98312 | tf_op jit(solution)/shard_map/ppermute | solution.py:21
Sparse Core Ops, SparseCore 0:
  15.9 655.3 all-reduce.4
  674.0 36.6 all-reduce.6
  785.5 46.8 all-reduce.8
